TPU v7x, 768 devices: a whole 4x8x12 slice. The times are simulated.
768 devices in a mesh: grp: 24 (over x, z_lo, core), freq: 32 (over y, z_hi).
Axes of the slice: x: 4, y: 8, z: 12 (z_hi: 4, z_lo: 3; z = z_hi * 3 + z_lo), core: 2. Of those that a mesh axis runs over, the one named last changes fastest.
Arguments:
- spectra: float32 [192, 2, 4096], P('grp', None, 'freq'), may hold values from -6 to 6
- station_mask: int32 [192], P('grp'), may hold values 0 or 1
- owners: int32 [24, 2, 64, 1], P('grp'), may hold values from 0 to 23; in each aligned block of 64 rows (0 to 63, 64 to 127, ..., all dimensions but the last counted through in order) at most 6 rows name the same one
Outputs:
- inbox: float32 [24, 2, 24, 6, 4096], P('grp', None, None, None, 'freq')
Inputs may be any that keep to these rules, and one draw needn't show every extreme that they name: `owners`: in each round, no owner is named by more than 6 of one group's 64 pairs, a bound that some block reaches; every group owns some pair.
All inputs are finite; a program needn't handle non-finite values. No bound on the sum of `station_mask` on one device may be relied on, other than what follows from the above.
Results may differ from a plain program's by a relative error of at most 0.0003.
Values sent between devices are 32-bit elements; how exact they have to be, the bound alone decides.
A program may use at most 32 MiB of HBM per device.

v0:
```python
import math

import jax
import jax.numpy as jnp
from jax import lax
from jax.sharding import PartitionSpec as P

LAGS = 4096


def passed_along(block, axis, distance):
    devices = range(lax.axis_size(axis))
    route = [((i - distance) % len(devices), i) for i in devices]
    return lax.ppermute(block, axis, route)


def phase_table(bin_ids, lag_count, bin_total):
    lag_ids = jnp.arange(lag_count, dtype=jnp.int32) - lag_count // 2
    phase_turns = jnp.mod(bin_ids[:, None] * lag_ids[None, :], 2 * bin_total)
    angles = phase_turns.astype(jnp.float32) * (math.pi / bin_total)
    return (jnp.cos(angles), jnp.sin(angles))


def per_device(spectra, station_mask, owners):
    station_count = spectra.shape[0]
    band_bins = spectra.shape[2]
    groups = lax.axis_size("grp")
    shards = lax.axis_size("freq")
    round_count = min(2, groups - 1)
    bin_total = band_bins * shards
    pair_count = station_count * station_count
    capacity = (2 * pair_count + groups - 1) // groups
    lag_band = LAGS // shards
    norm_scale = 1.0 / math.sqrt(bin_total)
    own_weight = station_mask.astype(jnp.float32)
    pair_ids = jnp.arange(pair_count, dtype=jnp.int32)
    earlier = pair_ids[None, :] < pair_ids[:, None]
    slot_ids = jnp.arange(groups * capacity, dtype=jnp.int32)
    first_bin = lax.axis_index("freq") * band_bins
    band_cos, band_sin = phase_table(
        first_bin + jnp.arange(band_bins, dtype=jnp.int32), LAGS, bin_total
    )
    lag_table = jnp.concatenate([band_cos, -band_sin], axis=0)
    held_spectra = spectra
    held_weight = own_weight
    buffers = []
    for round_index in range(round_count):
        held_spectra, held_weight = passed_along((spectra, own_weight), "grp", round_index + 1)
        pair_weight = (own_weight[:, None] * held_weight[None, :])[..., None]
        cross_real = (
            spectra[:, None, 0] * held_spectra[None, :, 0]
            + spectra[:, None, 1] * held_spectra[None, :, 1]
        ) * pair_weight
        cross_imag = (
            spectra[:, None, 1] * held_spectra[None, :, 0]
            - spectra[:, None, 0] * held_spectra[None, :, 1]
        ) * pair_weight
        cross_real = cross_real.reshape(pair_count, band_bins)
        cross_imag = cross_imag.reshape(pair_count, band_bins)
        flattened = jnp.concatenate([cross_real, cross_imag], axis=1)
        correlation = (
            lax.psum_scatter(
                jnp.einsum("kl,pk->lp", lag_table, flattened, precision=lax.Precision.HIGHEST),
                "freq",
                scatter_dimension=0,
                tiled=True,
            )
            * norm_scale
        )
        owner_ids = owners[0, round_index, :, 0]
        same_owner = (owner_ids[:, None] == owner_ids[None, :]) & earlier
        pair_rank = jnp.sum(same_owner.astype(jnp.int32), axis=1)
        placing = ((owner_ids * capacity + pair_rank)[:, None] == slot_ids[None, :]).astype(
            jnp.float32
        )
        buffers.append(
            jnp.einsum("lp,px->xl", correlation, placing, precision=lax.Precision.HIGHEST)
        )
    outgoing = jnp.stack(buffers, axis=0).reshape(round_count, groups, capacity, lag_band)
    incoming = lax.all_to_all(outgoing, "grp", split_axis=1, concat_axis=1, tiled=True)
    return incoming.reshape(1, round_count, groups, capacity, lag_band)


def solution(mesh):
    placed = (P("grp", None, "freq"), P("grp"), P("grp", None, None, None))
    return jax.shard_map(
        per_device,
        mesh=mesh,
        in_specs=placed,
        out_specs=P("grp", None, None, None, "freq"),
        check_vma=False,
    )
```

profile of v0, /device:TPU:1, one launch (start us, length us, event | category | flops | bytes accessed | tf_op | source)
XLA Modules:
  0.0 545.9 jit_solution(14262431070505491260)
XLA Ops:
  6.5 0.0 reduce-scatter.3.cloned.1.call-start
  6.5 0.7 convert_element_type.16
  7.2 5.4 collective-permute-start.1
  12.6 4.0 collective-permute-start.3
  16.6 2.2 collective-permute-start
  18.8 1.9 collective-permute-start.2
  20.7 0.8 fusion.27
  21.5 0.1 mul.241
  21.6 0.1 mul.242
  21.6 9.4 %fusion.5 = (f32[128,4096]{1,0:T(8,128)S(1)}, f32[128,4096]{1,0:T(8,128)}) fusion(s32[4096]{0:T(1024)S(1)} %iota_add_fusion, s32[128]{0:T(128)S(1)} %iota_add_fusion.1), kind=kLoop, calls=%fused_computation.12 | loop fusion | flops 7864320 | bytes 4211200 | tf_op jit(solution)/shard_map/cos | solution.py:21
  31.0 0.0 collective-permute-done.1
  31.0 0.1 mul.244
  31.1 0.0 collective-permute-done.3
  31.1 0.1 mul.260
  31.2 0.0 collective-permute-done
  31.2 0.0 collective-permute-done.2
  31.2 0.1 bitcast_multiply_fusion.3
  31.3 5.4 fusion.1
  36.7 0.0 reduce-scatter.3.cloned.1.call-update
  36.8 0.0 reduce-scatter.5.cloned.1.call-start
  36.8 0.0 copy-start
  36.8 5.4 fusion
  42.2 0.0 reduce-scatter.5.cloned.1.call-update
  42.3 0.0 copy-done
  42.3 0.2 convert_reduce_fusion
  42.5 236.1 %reduce-scatter.3.cloned.1.call-done = f32[128,64]{0,1:T(8,128)} async-done(((f32[4096,64]{0,1:T(8,128)}), f32[128,64]{0,1:T(8,128)}) %reduce-scatter.3.cloned.1.call-update) | async-done | bytes 32784 | tf_op jit(solution)/shard_map/reduce_scatter | solution.py:62
  278.6 1.1 fusion.12
  279.7 239.3 %reduce-scatter.5.cloned.1.call-done = f32[128,64]{0,1:T(8,128)} async-done(((f32[4096,64]{0,1:T(8,128)}), f32[128,64]{0,1:T(8,128)}) %reduce-scatter.5.cloned.1.call-update) | async-done | bytes 32784 | tf_op jit(solution)/shard_map/reduce_scatter | solution.py:62
  519.0 1.1 fusion.13
  520.1 0.1 copy.9
  520.2 18.2 %all_to_all.5 = f32[2,24,6,128]{3,0,2,1:T(2,128)S(1)} all-to-all(f32[2,24,6,128]{3,0,2,1:T(2,128)S(1)} %copy.9), channel_id=1, replica_groups=mesh['grp'=24,'freq'=32] {'grp'}, dimensions={1} | all-to-all | bytes 294912 | tf_op jit(solution)/shard_map/all_to_all | solution.py:80
  538.4 0.7 copy.10
  (12 shorter events, 0.1 us)
Async XLA Ops:
  6.5 272.0 %reduce-scatter.3.cloned.1.call-start = ((), (), s32[]{:S(2)}) async-start(), calls=%async_computation.3 | async-start | bytes 1081344 | tf_op jit(solution)/shard_map/reduce_scatter | solution.py:62
  7.2 23.8 %collective-permute-start.1 = (f32[8]{0:T(128)S(1)}, f32[8]{0:T(128)S(1)}, u32[]{:S(2)}, u32[]{:S(2)}) collective-permute-start(f32[8]{0:T(128)S(1)} %convert_element_type.16), channel_id=1, source_target_pairs={{736,0},{0,32},{32,64},{64,96},{96,128},{128,160},{160,192},{192,2... | collective-permute-start | bytes 104 | tf_op jit(solution)/shard_map/ppermute | solution.py:14
  12.6 18.5 %collective-permute-start.3 = (f32[8]{0:T(128)S(1)}, f32[8]{0:T(128)S(1)}, u32[]{:S(2)}, u32[]{:S(2)}) collective-permute-start(f32[8]{0:T(128)S(1)} %convert_element_type.16), channel_id=1, source_target_pairs={{704,0},{736,32},{0,64},{32,96},{64,128},{96,160},{128,192},{160,2... | collective-permute-start | bytes 104 | tf_op jit(solution)/shard_map/ppermute | solution.py:14
  16.6 14.6 %collective-permute-start = (f32[8,2,128]{2,1,0:T(2,128)}, f32[8,2,128]{2,1,0:T(2,128)S(1)}, u32[]{:S(2)}, u32[]{:S(2)}) collective-permute-start(f32[8,2,128]{2,1,0:T(2,128)} %param.3), channel_id=1, source_target_pairs={{736,0},{0,32},{32,64},{64,96},{96,128},{128,160},{160,192},{192,2... | collective-permute-start | bytes 24584 | tf_op jit(solution)/shard_map/ppermute | solution.py:14
  18.8 12.4 %collective-permute-start.2 = (f32[8,2,128]{2,1,0:T(2,128)}, f32[8,2,128]{2,1,0:T(2,128)S(1)}, u32[]{:S(2)}, u32[]{:S(2)}) collective-permute-start(f32[8,2,128]{2,1,0:T(2,128)} %param.3), channel_id=1, source_target_pairs={{704,0},{736,32},{0,64},{32,96},{64,128},{96,160},{128,192},{160,2... | collective-permute-start | bytes 24584 | tf_op jit(solution)/shard_map/ppermute | solution.py:14
  36.8 482.2 %reduce-scatter.5.cloned.1.call-start = ((), (), s32[]{:S(2)}) async-start(), calls=%async_computation.4 | async-start | bytes 1081344 | tf_op jit(solution)/shard_map/reduce_scatter | solution.py:62
  36.8 5.4 copy-start
Sparse Core Ops, SparseCore 0:
  36.9 241.6 reduce-scatter.2
  283.6 235.3 reduce-scatter.4
where the time goes:
time: 546 us
  waiting for transfers between devices  475 us (87%)
  blocking collectives  18.2 us (3%)
  between operations  13.6 us (2%)
  starting transfers between devices  13.5 us (2%)
  matrix products  13 us (2%)
  other arithmetic  10.3 us (2%)
    reduce_scatter x2, waiting for transfers between devices, per_device(): lax.psum_scatter(jnp.einsum('kl,pk->lp', lag_table, flattened, precision=...  475 us
    all_to_all x1, blocking collectives, per_device(): lax.all_to_all(outgoing, 'grp', split_axis=1, concat_axis=1, tiled=True)  18.2 us
    ppermute x4, starting transfers between devices, passed_along(): return lax.ppermute(block, axis, route)  13.5 us
  transfers between devices with their start and end apart: 6, of which 2 were waited for; matrix products, arithmetic and copies ran while one was open for 3% of the time, Pallas kernels for 0%

commit v1 on v0

v1 whole, which is shorter than its diff:
```python
import functools
import math

import jax
import jax.numpy as jnp
from jax import lax
from jax.experimental import pallas as pl
from jax.experimental.pallas import tpu as pltpu
from jax.sharding import PartitionSpec as P

LAGS_PER = 128
STA = 8
PAIRS = STA * STA
ROUNDS = 2
ZH = 4
MESH = pl.DeviceIdType.MESH
F32 = jnp.float32
BF16 = jnp.bfloat16


def split(v):
    hi = v.astype(BF16)
    return hi, (v - hi.astype(F32)).astype(BF16)


def kernel(
    dims, x_ref, slot_ref, cos_ref, sin_ref, out_ref,
    buf, tab, xb, acc, sbuf, rbuf,
    own_sem, z_send, z_recv, y_send, y_recv, f_send, f_recv, a_send, a_recv,
):
    G, Y, Z, cap, capp = dims
    BINS = 128
    HALF = Z * BINS
    g = lax.axis_index("grp")
    f = lax.axis_index("freq")
    y = f // Z
    zh = lax.rem(f, Z)
    right = lax.rem(g + 1, G)

    def zpeer(d):
        return (g, y * Z + lax.rem(zh + d, Z))

    def ypeer(d):
        return (g, lax.rem(y + d, Y) * Z + zh)

    def gpeer(d):
        return (lax.rem(g + d, G), f)

    barrier = pltpu.get_barrier_semaphore()
    for d in range(1, Z):
        pl.semaphore_signal(barrier, inc=1, device_id=zpeer(d), device_id_type=MESH)

    @pl.loop(1, Y)
    def _(d):
        pl.semaphore_signal(barrier, inc=1, device_id=ypeer(d), device_id_type=MESH)

    @pl.loop(1, G)
    def _(d):
        pl.semaphore_signal(barrier, inc=1, device_id=gpeer(d), device_id_type=MESH)

    def rel(s):
        return jnp.where(lax.rem(s, 2) == 1, (s + 1) // 2, lax.rem(Y - s // 2, Y))

    base_cos = cos_ref[0:BINS, :]
    base_sin = sin_ref[0:BINS, :]

    @pl.loop(0, Y)
    def _(s):
        first = BINS + lax.rem(y + rel(s), Y) * Z
        for j in range(Z):
            ec = cos_ref[pl.ds(first + j, 1), :]
            es = sin_ref[pl.ds(first + j, 1), :]
            c = base_cos * ec - base_sin * es
            n = -(base_sin * ec + base_cos * es)
            rows = pl.ds(j * BINS, BINS)
            hi, lo = split(c)
            tab[s, rows, 0:LAGS_PER] = hi
            tab[s, rows, LAGS_PER:2 * LAGS_PER] = lo
            rows = pl.ds(HALF + j * BINS, BINS)
            hi, lo = split(n)
            tab[s, rows, 0:LAGS_PER] = hi
            tab[s, rows, LAGS_PER:2 * LAGS_PER] = lo

    pl.semaphore_wait(barrier, (Z - 1) + (Y - 1) + (G - 1))

    def z_copy(d):
        return pltpu.make_async_remote_copy(
            src_ref=x_ref, dst_ref=buf.at[0, y, zh],
            send_sem=z_send.at[d - 1], recv_sem=z_recv.at[d - 1],
            device_id=zpeer(d), device_id_type=MESH)

    def z_arrival(d):
        band = buf.at[0, y, lax.rem(zh + Z - d, Z)]
        return pltpu.make_async_remote_copy(
            src_ref=band, dst_ref=band,
            send_sem=z_send.at[d - 1], recv_sem=z_recv.at[d - 1],
            device_id=zpeer(d), device_id_type=MESH)

    def y_copy(d, j, src):
        return pltpu.make_async_remote_copy(
            src_ref=src, dst_ref=buf.at[0, y, lax.rem(zh + Z - d, Z)],
            send_sem=y_send.at[d, j], recv_sem=y_recv.at[d, j],
            device_id=ypeer(j), device_id_type=MESH)

    def y_arrival(d, row, j):
        band = buf.at[0, row, lax.rem(zh + Z - d, Z)]
        return pltpu.make_async_remote_copy(
            src_ref=band, dst_ref=band,
            send_sem=y_send.at[d, j], recv_sem=y_recv.at[d, j],
            device_id=ypeer(j), device_id_type=MESH)

    def f_copy(hop, s):
        row = lax.rem(y + rel(s), Y)
        return pltpu.make_async_remote_copy(
            src_ref=buf.at[hop, row], dst_ref=buf.at[hop + 1, row],
            send_sem=f_send.at[hop, s], recv_sem=f_recv.at[hop, s],
            device_id=(right, f), device_id_type=MESH)

    def a_copy(d):
        return pltpu.make_async_remote_copy(
            src_ref=sbuf.at[lax.rem(g + d, G)], dst_ref=rbuf.at[g],
            send_sem=a_send.at[d], recv_sem=a_recv.at[d],
            device_id=gpeer(d), device_id_type=MESH)

    own = pltpu.make_async_copy(x_ref, buf.at[0, y, zh], own_sem)
    own.start()
    order = sorted(range(1, Z), key=lambda d: -min(d, Z - d))
    for d in order:
        z_copy(d).start()
    for j in sorted(range(1, Y), key=lambda j: -min(j, Y - j)):
        y_copy(0, j, x_ref).start()
    acc[...] = jnp.zeros_like(acc)
    for d in reversed(order):
        z_arrival(d).wait_recv()
        src = buf.at[0, y, lax.rem(zh + Z - d, Z)]
        for j in sorted(range(1, Y), key=lambda j: -min(j, Y - j)):
            y_copy(d, j, src).start()
    own.wait()

    def product(s):
        row = lax.rem(y + rel(s), Y)
        for b in range(Z):
            are = buf[0, row, b, 0]
            aim = buf[0, row, b, 1]
            for r in range(ROUNDS):
                bre = buf[r + 1, row, b, 0][None, :, :]
                bim = buf[r + 1, row, b, 1][None, :, :]
                re = are[:, None, :] * bre + aim[:, None, :] * bim
                im = aim[:, None, :] * bre - are[:, None, :] * bim
                for part, v in ((0, re), (1, im)):
                    hi, lo = split(v.reshape(PAIRS, BINS))
                    cols = pl.ds(part * HALF + b * BINS, BINS)
                    xb[r * PAIRS:(r + 1) * PAIRS, cols] = hi
                    xb[(ROUNDS + r) * PAIRS:(ROUNDS + r + 1) * PAIRS, cols] = lo
        acc[...] += jnp.dot(xb[...], tab[s], preferred_element_type=F32)

    @pl.loop(0, Y + 2)
    def _(t):
        @pl.when((t > 0) & (t < Y))
        def _():
            row = lax.rem(y + rel(t), Y)
            j = Y - rel(t)
            for d in range(Z):
                y_arrival(d, row, j).wait_recv()

        @pl.when(t < Y)
        def _():
            f_copy(0, t).start()

        @pl.when((t >= 1) & (t <= Y))
        def _():
            f_copy(0, t - 1).wait_recv()
            f_copy(1, t - 1).start()

        @pl.when(t >= 2)
        def _():
            f_copy(1, t - 2).wait_recv()
            product(t - 2)

    whole = (acc[0:128, 0:128] + acc[0:128, 128:256]
             + acc[128:256, 0:128] + acc[128:256, 128:256])
    whole = whole * (1.0 / math.sqrt(Y * Z * BINS))
    hi, lo = split(whole)
    slots = lax.broadcasted_iota(jnp.int32, (G * capp, PAIRS), 0)
    for r in range(ROUNDS):
        place = jnp.where(slots == slot_ref[r:r + 1, :], 1.0, 0.0).astype(BF16)
        rows = slice(r * PAIRS, (r + 1) * PAIRS)
        got = jnp.dot(place, hi[rows], preferred_element_type=F32) + jnp.dot(
            place, lo[rows], preferred_element_type=F32)
        sbuf[:, r] = got.reshape(G, capp, LAGS_PER)

    @pl.loop(1, G)
    def _(d):
        a_copy(d).start()

    out_ref[0, :, g] = sbuf[g, :, 0:cap]

    for d in range(1, Z):
        z_copy(d).wait_send()

    @pl.loop(1, Y)
    def _(j):
        for d in range(Z):
            y_copy(d, j, x_ref).wait_send()

    @pl.loop(0, Y)
    def _(s):
        for hop in range(2):
            f_copy(hop, s).wait_send()

    @pl.loop(1, G)
    def _(d):
        src = lax.rem(g + G - d, G)
        block = rbuf.at[src]
        pltpu.make_async_remote_copy(
            src_ref=block, dst_ref=block,
            send_sem=a_send.at[d], recv_sem=a_recv.at[d],
            device_id=gpeer(d), device_id_type=MESH).wait_recv()
        out_ref[0, :, src] = rbuf[src, :, 0:cap]

    @pl.loop(1, G)
    def _(d):
        a_copy(d).wait_send()


def per_device(Z, spectra, station_mask, owners):
    G = lax.axis_size("grp")
    F = lax.axis_size("freq")
    Y = F // Z
    NF = F * 128
    cap = (2 * PAIRS + G - 1) // G
    capp = -(-cap // 8) * 8
    own = spectra.transpose(1, 0, 2) * station_mask.astype(F32)[None, :, None]
    ids = owners[0, :, :, 0]
    p = jnp.arange(PAIRS, dtype=jnp.int32)
    same = (ids[:, :, None] == ids[:, None, :]) & (p[:, None] < p[None, :])[None]
    slot = ids * capp + jnp.sum(same.astype(jnp.int32), axis=1)
    m = lax.axis_index("freq") * 128 + jnp.arange(128, dtype=jnp.int32) - NF // 2
    k = jnp.arange(128 + F, dtype=jnp.int32)
    k = jnp.where(k < 128, k, (k - 128) * 128)
    angle = jnp.mod(k[:, None] * m[None, :], 2 * NF).astype(F32) * (math.pi / NF)
    vm = pl.BlockSpec(memory_space=pltpu.VMEM)
    dma = pltpu.SemaphoreType.DMA
    return pl.pallas_call(
        functools.partial(kernel, (G, Y, Z, cap, capp)),
        out_shape=jax.ShapeDtypeStruct((1, ROUNDS, G, cap, 128), F32),
        in_specs=[vm] * 4,
        out_specs=vm,
        scratch_shapes=[
            pltpu.VMEM((ROUNDS + 1, Y, Z, 2, STA, 128), F32),
            pltpu.VMEM((Y, 2 * Z * 128, 256), BF16),
            pltpu.VMEM((256, 2 * Z * 128), BF16),
            pltpu.VMEM((256, 256), F32),
            pltpu.VMEM((G, ROUNDS, capp, 128), F32),
            pltpu.VMEM((G, ROUNDS, capp, 128), F32),
            dma, dma((Z - 1,)), dma((Z - 1,)),
            dma((Z, Y)), dma((Z, Y)),
            dma((2, Y)), dma((2, Y)),
            dma((G,)), dma((G,)),
        ],
        compiler_params=pltpu.CompilerParams(
            collective_id=0, has_side_effects=True, vmem_limit_bytes=32 << 20),
    )(own, slot, jnp.cos(angle), jnp.sin(angle))


def solution(mesh):
    placed = (P("grp", None, "freq"), P("grp"), P("grp", None, None, None))
    return jax.shard_map(
        functools.partial(per_device, ZH),
        mesh=mesh,
        in_specs=placed,
        out_specs=P("grp", None, None, None, "freq"),
        check_vma=False,
    )
```

time: 546 us -> 50.1 us (0.09)
  waiting for transfers between devices: 475 us -> 0 us
  Pallas kernels: 0 us -> 47.3 us
  blocking collectives: 18.2 us -> 0 us
  between operations: 13.6 us -> 0.03 us
  starting transfers between devices: 13.5 us -> 0 us
  matrix products: 13 us -> 0 us
  other arithmetic: 10.3 us -> 0.59 us
    reduce_scatter x2 -> x0, waiting for transfers between devices: 475 us -> none  [per_device(): lax.psum_scatter(jnp.einsum('kl,pk->lp', lag_table, flattened, precision=...]
    pallas_call x0 -> x1, Pallas kernels: none -> 47.3 us  [per_device(): pl.pallas_call(functools.partial(kernel, (G, Y, Z, cap, capp)), out_shape...]
    all_to_all x1 -> x0, blocking collectives: 18.2 us -> none  [per_device(): lax.all_to_all(outgoing, 'grp', split_axis=1, concat_axis=1, tiled=True)]
    ppermute x4 -> x0, starting transfers between devices: 13.5 us -> none  [passed_along(): return lax.ppermute(block, axis, route)]
    dot_general x4 -> x0, matrix products: 13 us -> none  [the longest x2 10.8 us: per_device(): jnp.einsum('kl,pk->lp', lag_table, flattened, precision=lax.Precision.HIG...]
    cos x1 -> x0, other arithmetic: 9.36 us -> none  [phase_table(): return (jnp.cos(angles), jnp.sin(angles))]
  transfers between devices with their start and end apart: 6 -> 0, of which waited for: 2 -> 0; matrix products, arithmetic and copies ran while one was open for 3% -> 0% of each run, Pallas kernels for 0% -> 0%
where the time goes in v1:
time: 50.1 us; the launch traced here: 49.9 us
  Pallas kernels  47.3 us (94%)
  local copies, waits for them, and re-layouts  2.03 us (4%)
  other arithmetic  0.59 us (1%)
    pallas_call x1, Pallas kernels, per_device(): pl.pallas_call(functools.partial(kernel, (G, Y, Z, cap, capp)), out_shape...  47.3 us
    unnamed x6, local copies, waits for them, and re-layouts  1.34 us

profile of v1, /device:TPU:1, one launch (start us, length us, event | category | flops | bytes accessed | tf_op | source)
XLA Modules:
  0.0 49.9 jit_solution(11880389362996336792)
XLA Ops:
  0.0 0.0 copy-start.1
  0.0 0.0 copy-start.2
  0.0 0.7 %copy-done.2 = s32[8]{0:T(128)S(1)} copy-done((s32[8]{0:T(128)S(1)}, s32[8]{0:T(128)}, u32[]{:S(2)}) %copy-start.2) | copy-done | bytes 56
  0.7 0.0 copy-done.1
  0.7 0.1 fusion.5.x_ref
  0.8 0.0 copy-start
  0.8 0.7 %copy-done = s32[1,2,64,1]{2,3,1,0:T(1,128)S(1)} copy-done((s32[1,2,64,1]{2,3,1,0:T(1,128)S(1)}, s32[1,2,64,1]{2,3,1,0:T(1,128)}, u32[]{:S(2)}) %copy-start) | copy-done | bytes 536
  1.4 0.1 convert_reduce_fusion
  1.6 0.4 fusion.3
  2.0 47.3 %shard_map.37 = f32[1,2,24,6,128]{4,3,2,1,0:T(8,128)S(1)} custom-call(f32[2,8,128]{2,1,0:T(8,128)S(1)} %fusion.5.x_ref, s32[2,64]{1,0:T(2,128)S(1)} %multiply_add_fusion.slot_ref, f32[160,128]{1,0:T(8,128)S(1)} %get-tuple-element.6.cos_ref, f32[160,128]{1,0:T(8,128)S(1)} %get-tuple-element.5.sin_ref), custom_call_target="tpu_custom_call" | custom-call | tf_op jit(solution)/shard_map/pallas_call | solution.py:244
  49.2 0.7 %copy.7 = f32[1,2,24,6,128]{4,2,3,1,0:T(8,128)} copy(f32[1,2,24,6,128]{4,3,2,1,0:T(8,128)S(1)} %shard_map.37) | data formatting | bytes 294912 | tf_op jit(solution)/shard_map/pallas_call | solution.py:244
  (5 shorter events, 0.0 us)
Async XLA Ops:
  0.0 0.7 %copy-start.1 = (f32[8,2,128]{2,1,0:T(2,128)S(1)}, f32[8,2,128]{2,1,0:T(2,128)}, u32[]{:S(2)}) copy-start(f32[8,2,128]{2,1,0:T(2,128)} %param.3) | copy-start | bytes 24580
  0.0 0.7 %copy-start.2 = (s32[8]{0:T(128)S(1)}, s32[8]{0:T(128)}, u32[]{:S(2)}) copy-start(s32[8]{0:T(128)} %param.4) | copy-start | bytes 100
  0.8 0.7 %copy-start = (s32[1,2,64,1]{2,3,1,0:T(1,128)S(1)}, s32[1,2,64,1]{2,3,1,0:T(1,128)}, u32[]{:S(2)}) copy-start(s32[1,2,64,1]{2,3,1,0:T(1,128)} %param.5) | copy-start | bytes 1540

commit v2 on v0

v2 whole, which is shorter than its diff:
```python
import functools
import math

import jax
import jax.numpy as jnp
from jax import lax
from jax.experimental import pallas as pl
from jax.experimental.pallas import tpu as pltpu
from jax.sharding import PartitionSpec as P

BINS = 128
STA = 8
PAIRS = STA * STA
ROUNDS = 2
Z = 4
CHIP_GROUPS = 6
UNITS = 2 * Z
PLACE = {1: 1, 3: 2, 2: 3}
MESH = pl.DeviceIdType.MESH
F32 = jnp.float32
BF16 = jnp.bfloat16


def split(v):
    hi = v.astype(BF16)
    return hi, (v - hi.astype(F32)).astype(BF16)


def trig(k, m, nf):
    angle = lax.rem(lax.rem(k * m, 2 * nf) + 2 * nf, 2 * nf).astype(F32) * (math.pi / nf)
    return jnp.cos(angle), jnp.sin(angle)


def kernel(
    dims, x_hbm, mask_hbm, owner_hbm, out_ref,
    xin, maskin, ownerin, place, phase, buf, tab, xb, acc, sbuf, rbuf,
    in_sem, z_send, z_recv, y_send, y_recv, f_send, f_recv, a_send, a_recv,
):
    G, Y, cap, capp = dims
    Q = Y // 2
    HALF = Q * BINS
    NF = Y * Z * BINS
    g = lax.axis_index("grp")
    f = lax.axis_index("freq")
    y = f // Z
    zh = lax.rem(f, Z)
    right = lax.rem(g + 1, G)
    per_x = CHIP_GROUPS if G % CHIP_GROUPS == 0 else 1
    X = G // per_x

    def zpeer(d):
        return (g, y * Z + lax.rem(zh + d, Z))

    def ypeer(d):
        return (g, lax.rem(y + d, Y) * Z + zh)

    def owner(i):
        turn = i // per_x
        dx = jnp.where(turn == X - 1, 0, lax.rem(X // 2 + jnp.where(
            lax.rem(turn, 2) == 1, X - (turn + 1) // 2, turn // 2), X))
        return lax.rem(g // per_x + dx, X) * per_x + lax.rem(i, per_x)

    barrier = pltpu.get_barrier_semaphore()

    def greet(peer):
        pl.semaphore_signal(barrier, inc=1, device_id=peer, device_id_type=MESH)

    greet(zpeer(1))
    greet(zpeer(Z - 1))

    @pl.loop(1, Y)
    def _(d):
        greet(ypeer(d))

    @pl.loop(1, G)
    def _(d):
        greet((lax.rem(g + d, G), f))

    loads = [
        pltpu.make_async_copy(a, b, in_sem.at[i])
        for i, (a, b) in enumerate(((x_hbm, xin), (mask_hbm, maskin), (owner_hbm, ownerin)))]
    for load in loads:
        load.start()

    lag = f * BINS + lax.broadcasted_iota(jnp.int32, (1, BINS), 1) - NF // 2
    base_cos, base_sin = trig(lax.broadcasted_iota(jnp.int32, (BINS, 1), 0), lag, NF)
    first_cos, first_sin = trig(
        BINS * lax.broadcasted_iota(jnp.int32, (Y * Z, 1), 0), lag, NF)
    phase[0] = first_cos
    phase[1] = first_sin
    for load in loads:
        load.wait()

    def column(row):
        n = row.shape[1]
        own = lax.broadcasted_iota(jnp.int32, (n, n), 0) == lax.broadcasted_iota(
            jnp.int32, (n, n), 1)
        return jnp.sum(jnp.where(own, row, 0.0), axis=1, keepdims=True)

    mask = column(maskin[...].astype(F32))
    buf[0, 0, 0, 0] = xin[:, 0, :] * mask
    buf[0, 0, 0, 1] = xin[:, 1, :] * mask
    for r in range(ROUNDS):
        row = ownerin[r:r + 1, :].astype(F32)
        ahead = lax.broadcasted_iota(jnp.int32, (PAIRS, PAIRS), 0) < lax.broadcasted_iota(
            jnp.int32, (PAIRS, PAIRS), 1)
        same = jnp.where(ahead & (column(row) == row), 1.0, 0.0)
        slot = row * capp + jnp.sum(same, axis=0, keepdims=True)
        slots = lax.broadcasted_iota(jnp.int32, (G * capp, PAIRS), 0).astype(F32)
        place[r] = jnp.where(slots == slot, 1.0, 0.0).astype(BF16)

    def rel(i):
        return jnp.where(lax.rem(i, 2) == 1, (i + 1) // 2, lax.rem(Y - i // 2, Y))

    @pl.loop(0, UNITS)
    def _(s):
        e = s // 2
        d = jnp.where(e == 2, 3, jnp.where(e == 3, 2, e))
        col = lax.rem(zh + Z - d, Z)
        for q in range(Q):
            band = lax.rem(y + rel(lax.rem(s, 2) * Q + q), Y) * Z + col
            ec = phase[0, pl.ds(band, 1), :]
            es = phase[1, pl.ds(band, 1), :]
            c = base_cos * ec - base_sin * es
            n = -(base_sin * ec + base_cos * es)
            for at, v in ((q * BINS, c), (HALF + q * BINS, n)):
                hi, lo = split(v)
                tab[s, at:at + BINS, 0:BINS] = hi
                tab[s, at:at + BINS, BINS:2 * BINS] = lo

    acc[...] = jnp.zeros_like(acc)
    pl.semaphore_wait(barrier, 2 + (Y - 1) + (G - 1))

    def remote(src, dst, ssem, rsem, peer):
        return pltpu.make_async_remote_copy(
            src_ref=src, dst_ref=dst, send_sem=ssem, recv_sem=rsem,
            device_id=peer, device_id_type=MESH)

    def z_copy(d):
        return remote(buf.at[0, 0, 0], buf.at[0, 2 * PLACE[d], 0],
                      z_send.at[PLACE[d] - 1], z_recv.at[PLACE[d] - 1], zpeer(d))

    def z_relay(d):
        part = 0 if d == 1 else 1
        return remote(buf.at[0, 2 * PLACE[d], 0, part], buf.at[0, 2 * PLACE[2], 0, part],
                      z_send.at[2 + part], z_recv.at[2 + part], zpeer(d))

    def y_copy(e, j):
        i = 2 * j if j < Y // 2 else 2 * (Y - j) - 1
        return remote(buf.at[0, 2 * e, 0], buf.at[0, 2 * e + i // Q, i % Q],
                      y_send.at[e, j], y_recv.at[e, i], ypeer(j))

    rows = sorted(range(1, Y), key=lambda j: -min(j, Y - j))

    def f_copy(hop, s):
        return remote(buf.at[hop, s], buf.at[hop + 1, s],
                      f_send.at[hop, s], f_recv.at[hop, s], (right, f))

    def a_copy(r, i):
        o = owner(i)
        return o, remote(sbuf.at[r, o], rbuf.at[r, g],
                         a_send.at[r, o], a_recv.at[r, g], (o, f))

    z_copy(1).start()
    z_copy(Z - 1).start()
    for j in rows:
        y_copy(0, j).start()
    for d in (1, Z - 1):
        z_copy(d).wait_recv()
        z_relay(d).start()
    for d in (1, Z - 1):
        for j in rows:
            y_copy(PLACE[d], j).start()

    def product(r, s):
        for q in range(Q):
            are = buf[0, s, q, 0]
            aim = buf[0, s, q, 1]
            bre = buf[r + 1, s, q, 0][None, :, :]
            bim = buf[r + 1, s, q, 1][None, :, :]
            re = are[:, None, :] * bre + aim[:, None, :] * bim
            im = aim[:, None, :] * bre - are[:, None, :] * bim
            for at, v in ((q * BINS, re), (HALF + q * BINS, im)):
                hi, lo = split(v.reshape(PAIRS, BINS))
                xb[0:PAIRS, at:at + BINS] = hi
                xb[PAIRS:2 * PAIRS, at:at + BINS] = lo
        acc[r] += jnp.dot(xb[...], tab[s], preferred_element_type=F32)

    def hand_out(r):
        whole = (acc[r, 0:PAIRS, 0:BINS] + acc[r, 0:PAIRS, BINS:2 * BINS]
                 + acc[r, PAIRS:2 * PAIRS, 0:BINS] + acc[r, PAIRS:2 * PAIRS, BINS:2 * BINS])
        hi, lo = split(whole * (1.0 / math.sqrt(NF)))
        got = jnp.dot(place[r], hi, preferred_element_type=F32) + jnp.dot(
            place[r], lo, preferred_element_type=F32)
        sbuf[r] = got.reshape(G, capp, BINS)

        @pl.loop(0, G)
        def _(i):
            o, copy = a_copy(r, i)

            @pl.when(o != g)
            def _():
                copy.start()

    @pl.loop(0, UNITS + 3)
    def _(t):
        @pl.when(t == 2)
        def _():
            for d in (1, Z - 1):
                z_relay(d).wait_recv()
            for j in rows:
                y_copy(PLACE[2], j).start()

        @pl.when(t < UNITS)
        def _():
            e = t // 2
            for q in range(Q):
                def arrive(q=q):
                    band = buf.at[0, t, q]
                    remote(band, band, y_send.at[0, 0],
                           y_recv.at[e, lax.rem(t, 2) * Q + q], (right, f)).wait_recv()
                if q == 0:
                    pl.when(lax.rem(t, 2) == 1)(arrive)
                else:
                    arrive()
            f_copy(0, t).start()

        @pl.when(t >= 3)
        def _():
            f_copy(0, t - 3).wait_recv()
            f_copy(1, t - 3).start()
            product(0, t - 3)

        @pl.when(t >= 5)
        def _():
            f_copy(1, t - 5).wait_recv()
            product(1, t - 5)

    hand_out(0)

    @pl.loop(UNITS - 2, UNITS)
    def _(s):
        f_copy(1, s).wait_recv()
        product(1, s)

    hand_out(1)
    for r in range(ROUNDS):
        out_ref[pl.ds(r * cap * G + g, cap, stride=G), :] = sbuf[r, g, 0:cap]

    for d in (1, Z - 1):
        z_copy(d).wait_send()
        z_relay(d).wait_send()
    for e in range(Z):
        for j in rows:
            y_copy(e, j).wait_send()

    @pl.loop(0, UNITS)
    def _(s):
        for hop in range(2):
            f_copy(hop, s).wait_send()

    for r in range(ROUNDS):
        @pl.loop(0, G)
        def _(src, r=r):
            @pl.when(src != g)
            def _():
                block = rbuf.at[r, src]
                copy = remote(block, block, a_send.at[r, src], a_recv.at[r, src], (src, f))
                copy.wait_recv()
                copy.wait_send()
                out_ref[pl.ds(r * cap * G + src, cap, stride=G), :] = rbuf[r, src, 0:cap]


def per_device(spectra, station_mask, owners):
    G = lax.axis_size("grp")
    F = lax.axis_size("freq")
    Y = F // Z
    cap = (2 * PAIRS + G - 1) // G
    capp = -(-cap // 8) * 8
    hbm = pl.BlockSpec(memory_space=pltpu.HBM)
    dma = pltpu.SemaphoreType.DMA
    vmem = pltpu.VMEM
    held = pl.pallas_call(
        functools.partial(kernel, (G, Y, cap, capp)),
        out_shape=jax.ShapeDtypeStruct((ROUNDS * cap * G, BINS), F32),
        in_specs=[hbm] * 3,
        out_specs=pl.BlockSpec(memory_space=vmem),
        scratch_shapes=[
            vmem((STA, 2, BINS), F32),
            vmem((1, STA), jnp.int32),
            vmem((ROUNDS, PAIRS), jnp.int32),
            vmem((ROUNDS, G * capp, PAIRS), BF16),
            vmem((2, F, BINS), F32),
            vmem((ROUNDS + 1, UNITS, Y // 2, 2, STA, BINS), F32),
            vmem((UNITS, Y * BINS, 2 * BINS), BF16),
            vmem((2 * PAIRS, Y * BINS), BF16),
            vmem((ROUNDS, 2 * PAIRS, 2 * BINS), F32),
            vmem((ROUNDS, G, capp, BINS), F32),
            vmem((ROUNDS, G, capp, BINS), F32),
            dma((3,)), dma((4,)), dma((4,)),
            dma((Z, Y)), dma((Z, Y)),
            dma((2, UNITS)), dma((2, UNITS)),
            dma((ROUNDS, G)), dma((ROUNDS, G)),
        ],
        compiler_params=pltpu.CompilerParams(
            collective_id=0, has_side_effects=True, vmem_limit_bytes=32 << 20),
    )(spectra, station_mask.reshape(1, STA), owners.reshape(ROUNDS, PAIRS))
    return held.reshape(1, ROUNDS, cap, G, BINS).transpose(0, 1, 3, 2, 4)


def solution(mesh):
    placed = (P("grp", None, "freq"), P("grp"), P("grp", None, None, None))
    return jax.shard_map(
        per_device,
        mesh=mesh,
        in_specs=placed,
        out_specs=P("grp", None, None, None, "freq"),
        check_vma=False,
    )
```

time: 546 us -> 45.4 us (0.08)
  waiting for transfers between devices: 475 us -> 0 us
  Pallas kernels: 0 us -> 43.1 us
  blocking collectives: 18.2 us -> 0 us
  between operations: 13.6 us -> 0.01 us
  starting transfers between devices: 13.5 us -> 0 us
  matrix products: 13 us -> 0 us
  other arithmetic: 10.3 us -> 0 us
    reduce_scatter x2 -> x0, waiting for transfers between devices: 475 us -> none  [per_device(): lax.psum_scatter(jnp.einsum('kl,pk->lp', lag_table, flattened, precision=...]
    pallas_call x0 -> x1, Pallas kernels: none -> 43.1 us  [per_device(): pl.pallas_call(functools.partial(kernel, (G, Y, cap, capp)), out_shape=ja...]
    all_to_all x1 -> x0, blocking collectives: 18.2 us -> none  [per_device(): lax.all_to_all(outgoing, 'grp', split_axis=1, concat_axis=1, tiled=True)]
    ppermute x4 -> x0, starting transfers between devices: 13.5 us -> none  [passed_along(): return lax.ppermute(block, axis, route)]
    dot_general x4 -> x0, matrix products: 13 us -> none  [the longest x2 10.8 us: per_device(): jnp.einsum('kl,pk->lp', lag_table, flattened, precision=lax.Precision.HIG...]
    cos x1 -> x0, other arithmetic: 9.36 us -> none  [phase_table(): return (jnp.cos(angles), jnp.sin(angles))]
  transfers between devices with their start and end apart: 6 -> 0, of which waited for: 2 -> 0; matrix products, arithmetic and copies ran while one was open for 3% -> 0% of each run, Pallas kernels for 0% -> 0%
where the time goes in v2:
time: 45.4 us; the launch traced here: 45.2 us
  Pallas kernels  43.1 us (95%)
  local copies, waits for them, and re-layouts  2.04 us (4%)
    pallas_call x1, Pallas kernels, per_device(): pl.pallas_call(functools.partial(kernel, (G, Y, cap, capp)), out_shape=ja...  43.1 us
    unnamed x7, local copies, waits for them, and re-layouts  2.04 us

profile of v2, /device:TPU:1, one launch (start us, length us, event | category | flops | bytes accessed | tf_op | source)
XLA Modules:
  0.0 45.2 jit_solution(4228809988778049826)
XLA Ops:
  0.0 0.0 copy-start.1
  0.0 0.0 copy-start.2
  0.0 0.7 %copy-done.1 = s32[1,2,64,1]{2,3,1,0:T(1,128)S(1)} copy-done((s32[1,2,64,1]{2,3,1,0:T(1,128)S(1)}, s32[1,2,64,1]{2,3,1,0:T(1,128)}, u32[]{:S(2)}) %copy-start.1) | copy-done | bytes 536
  0.7 0.0 copy-done.2
  0.7 0.0 copy-start
  0.7 0.7 %copy-done = f32[8,2,128]{2,1,0:T(2,128)S(1)} copy-done((f32[8,2,128]{2,1,0:T(2,128)S(1)}, f32[8,2,128]{2,1,0:T(2,128)}, u32[]{:S(2)}) %copy-start) | copy-done | bytes 8216
  1.4 43.1 %shard_map.37 = f32[288,128]{1,0:T(8,128)S(1)} custom-call(f32[8,2,128]{2,1,0:T(2,128)S(1)} %copy-done, s32[1,8]{1,0:T(1,128)S(1)} %bitcast.7, s32[2,64]{1,0:T(2,128)S(1)} %bitcast.6), custom_call_target="tpu_custom_call" | custom-call | tf_op jit(solution)/shard_map/pallas_call | solution.py:283
  44.5 0.7 %copy.5 = f32[1,2,24,6,128]{4,2,3,1,0:T(8,128)} copy(f32[1,2,24,6,128]{4,2,3,1,0:T(8,128)S(1)} %bitcast.5) | data formatting | bytes 294912
Async XLA Ops:
  0.0 0.7 %copy-start.1 = (s32[1,2,64,1]{2,3,1,0:T(1,128)S(1)}, s32[1,2,64,1]{2,3,1,0:T(1,128)}, u32[]{:S(2)}) copy-start(s32[1,2,64,1]{2,3,1,0:T(1,128)} %param.5) | copy-start | bytes 1540
  0.0 0.7 %copy-start.2 = (s32[8]{0:T(128)S(1)}, s32[8]{0:T(128)}, u32[]{:S(2)}) copy-start(s32[8]{0:T(128)} %param.4) | copy-start | bytes 100
  0.7 0.7 %copy-start = (f32[8,2,128]{2,1,0:T(2,128)S(1)}, f32[8,2,128]{2,1,0:T(2,128)}, u32[]{:S(2)}) copy-start(f32[8,2,128]{2,1,0:T(2,128)} %x_hbm.1) | copy-start | bytes 24580

commit v3 on v2

v3 whole, which is shorter than its diff:
```python
import functools
import math

import jax
import jax.numpy as jnp
from jax import lax
from jax.experimental import pallas as pl
from jax.experimental.pallas import tpu as pltpu
from jax.sharding import PartitionSpec as P

BINS = 128
STA = 8
PAIRS = STA * STA
ROUNDS = 2
LAG = 4
Z = 4
CHIP_GROUPS = 6
UNITS = 2 * Z
PLACE = {1: 1, 3: 2, 2: 3}
MESH = pl.DeviceIdType.MESH
F32 = jnp.float32
BF16 = jnp.bfloat16


def split(v):
    hi = v.astype(BF16)
    return hi, (v - hi.astype(F32)).astype(BF16)


def trig(k, m, nf):
    angle = lax.rem(lax.rem(k * m, 2 * nf) + 2 * nf, 2 * nf).astype(F32) * (math.pi / nf)
    return jnp.cos(angle), jnp.sin(angle)


def kernel(
    dims, x_hbm, mask_hbm, owner_hbm, out_ref,
    xin, maskin, ownerin, place, phase, buf, tab, xb, acc, sbuf, rbuf,
    in_sem, z_send, z_recv, y_send, y_recv, f_send, f_recv, a_send, a_recv,
):
    G, Y, cap, capp = dims
    Q = Y // 2
    HALF = Q * BINS
    NF = Y * Z * BINS
    g = lax.axis_index("grp")
    f = lax.axis_index("freq")
    y = f // Z
    zh = lax.rem(f, Z)
    right = lax.rem(g + 1, G)
    per_x = CHIP_GROUPS if G % CHIP_GROUPS == 0 else 1
    X = G // per_x

    def zpeer(d):
        return (g, y * Z + lax.rem(zh + d, Z))

    def ypeer(d):
        return (g, lax.rem(y + d, Y) * Z + zh)

    turns = sorted(range(X), key=lambda dx: -min(dx, X - dx))
    mine = lax.rem(g, per_x)

    def along(dx, b):
        return lax.rem(g // per_x + dx, X) * per_x + b

    def other(o, dx, do):
        if dx == 0:
            pl.when(o != g)(do)
        else:
            do()

    barrier = pltpu.get_barrier_semaphore()

    def greet(peer):
        pl.semaphore_signal(barrier, inc=1, device_id=peer, device_id_type=MESH)

    greet(zpeer(1))
    greet(zpeer(Z - 1))

    @pl.loop(1, Y)
    def _(d):
        greet(ypeer(d))

    @pl.loop(1, G)
    def _(d):
        greet((lax.rem(g + d, G), f))

    loads = [
        pltpu.make_async_copy(a, b, in_sem.at[i])
        for i, (a, b) in enumerate(((x_hbm, xin), (mask_hbm, maskin), (owner_hbm, ownerin)))]
    for load in loads:
        load.start()

    for load in loads:
        load.wait()

    def column(row):
        n = row.shape[1]
        own = lax.broadcasted_iota(jnp.int32, (n, n), 0) == lax.broadcasted_iota(
            jnp.int32, (n, n), 1)
        return jnp.sum(jnp.where(own, row, 0.0), axis=1, keepdims=True)

    mask = column(maskin[...].astype(F32))
    buf[0, 0, 0, 0] = xin[:, 0, :] * mask
    buf[0, 0, 0, 1] = xin[:, 1, :] * mask
    def rel(i):
        return jnp.where(lax.rem(i, 2) == 1, (i + 1) // 2, lax.rem(Y - i // 2, Y))

    pl.semaphore_wait(barrier, 2 + (Y - 1) + (G - 1))

    def remote(src, dst, ssem, rsem, peer):
        return pltpu.make_async_remote_copy(
            src_ref=src, dst_ref=dst, send_sem=ssem, recv_sem=rsem,
            device_id=peer, device_id_type=MESH)

    def z_copy(d):
        return remote(buf.at[0, 0, 0], buf.at[0, 2 * PLACE[d], 0],
                      z_send.at[PLACE[d] - 1], z_recv.at[PLACE[d] - 1], zpeer(d))

    def z_relay(d):
        part = 0 if d == 1 else 1
        return remote(buf.at[0, 2 * PLACE[d], 0, part], buf.at[0, 2 * PLACE[2], 0, part],
                      z_send.at[2 + part], z_recv.at[2 + part], zpeer(d))

    def y_copy(e, j):
        i = 2 * j if j < Y // 2 else 2 * (Y - j) - 1
        return remote(buf.at[0, 2 * e, 0], buf.at[0, 2 * e + i // Q, i % Q],
                      y_send.at[e, j], y_recv.at[e, i], ypeer(j))

    rows = sorted(range(1, Y), key=lambda j: -min(j, Y - j))

    def f_copy(hop, s):
        return remote(buf.at[0, s], buf.at[hop + 1, s], f_send.at[hop, s],
                      f_recv.at[hop, s], (lax.rem(g + 1 + hop, G), f))

    def a_copy(dx, b):
        o = along(dx, b)
        return o, remote(sbuf.at[o], rbuf.at[g], a_send.at[dx * per_x + b],
                         a_recv.at[dx * per_x + mine], (o, f))

    z_copy(1).start()
    z_copy(Z - 1).start()
    for j in rows:
        y_copy(0, j).start()
    lag = f * BINS + lax.broadcasted_iota(jnp.int32, (1, BINS), 1) - NF // 2
    base_cos, base_sin = trig(lax.broadcasted_iota(jnp.int32, (BINS, 1), 0), lag, NF)
    first_cos, first_sin = trig(
        BINS * lax.broadcasted_iota(jnp.int32, (Y * Z, 1), 0), lag, NF)
    phase[0] = first_cos
    phase[1] = first_sin
    def table(s):
        e = s // 2
        d = jnp.where(e == 2, 3, jnp.where(e == 3, 2, e))
        col = lax.rem(zh + Z - d, Z)
        for q in range(Q):
            band = lax.rem(y + rel(lax.rem(s, 2) * Q + q), Y) * Z + col
            ec = phase[0, pl.ds(band, 1), :]
            es = phase[1, pl.ds(band, 1), :]
            c = base_cos * ec - base_sin * es
            n = -(base_sin * ec + base_cos * es)
            for at, v in ((q * BINS, c), (HALF + q * BINS, n)):
                hi, lo = split(v)
                tab[s, at:at + BINS, 0:BINS] = hi
                tab[s, at:at + BINS, BINS:2 * BINS] = lo

    pl.loop(0, UNITS // 2)(table)
    acc[...] = jnp.zeros_like(acc)
    for d in (1, Z - 1):
        z_copy(d).wait_recv()
        z_relay(d).start()
    for d in (1, Z - 1):
        for j in rows:
            y_copy(PLACE[d], j).start()
    pl.loop(UNITS // 2, UNITS)(table)

    for r in range(ROUNDS):
        row = ownerin[r:r + 1, :].astype(F32)
        ahead = lax.broadcasted_iota(jnp.int32, (PAIRS, PAIRS), 0) < lax.broadcasted_iota(
            jnp.int32, (PAIRS, PAIRS), 1)
        same = jnp.where(ahead & (column(row) == row), 1.0, 0.0)
        slot = row * capp + jnp.sum(same, axis=0, keepdims=True)
        slots = lax.broadcasted_iota(jnp.int32, (G * capp, PAIRS), 0).astype(F32)
        place[r] = jnp.where(slots == slot, 1.0, 0.0).astype(BF16)


    def product(s):
        for q in range(Q):
            are = buf[0, s, q, 0]
            aim = buf[0, s, q, 1]
            for r in range(ROUNDS):
                bre = buf[r + 1, s, q, 0][None, :, :]
                bim = buf[r + 1, s, q, 1][None, :, :]
                re = are[:, None, :] * bre + aim[:, None, :] * bim
                im = aim[:, None, :] * bre - are[:, None, :] * bim
                for at, v in ((q * BINS, re), (HALF + q * BINS, im)):
                    hi, lo = split(v.reshape(PAIRS, BINS))
                    xb[2 * r * PAIRS:(2 * r + 1) * PAIRS, at:at + BINS] = hi
                    xb[(2 * r + 1) * PAIRS:(2 * r + 2) * PAIRS, at:at + BINS] = lo
        acc[...] += jnp.dot(xb[...], tab[s], preferred_element_type=F32)

    @pl.loop(0, UNITS + LAG)
    def _(t):
        @pl.when(t == 2)
        def _():
            for d in (1, Z - 1):
                z_relay(d).wait_recv()
            for j in rows:
                y_copy(PLACE[2], j).start()

        @pl.when(t < UNITS)
        def _():
            e = t // 2
            for q in range(Q):
                def arrive(q=q):
                    band = buf.at[0, t, q]
                    remote(band, band, y_send.at[0, 0],
                           y_recv.at[e, lax.rem(t, 2) * Q + q], (right, f)).wait_recv()
                if q == 0:
                    pl.when(lax.rem(t, 2) == 1)(arrive)
                else:
                    arrive()
            f_copy(0, t).start()
            f_copy(1, t).start()

        @pl.when(t >= LAG)
        def _():
            f_copy(0, t - LAG).wait_recv()
            f_copy(1, t - LAG).wait_recv()
            product(t - LAG)

    for r in range(ROUNDS):
        top, low = 2 * r * PAIRS, (2 * r + 1) * PAIRS
        whole = (acc[top:low, 0:BINS] + acc[top:low, BINS:2 * BINS]
                 + acc[low:low + PAIRS, 0:BINS] + acc[low:low + PAIRS, BINS:2 * BINS])
        hi, lo = split(whole * (1.0 / math.sqrt(NF)))
        got = jnp.dot(place[r], hi, preferred_element_type=F32) + jnp.dot(
            place[r], lo, preferred_element_type=F32)
        sbuf[:, r] = got.reshape(G, capp, BINS)[:, 0:cap]
    for dx in turns:
        for b in range(per_x):
            o, copy = a_copy(dx, b)
            other(o, dx, copy.start)
    for r in range(ROUNDS):
        out_ref[pl.ds(r * cap * G + g, cap, stride=G), :] = sbuf[g, r]

    for d in (1, Z - 1):
        z_copy(d).wait_send()
        z_relay(d).wait_send()
    for e in range(Z):
        for j in rows:
            y_copy(e, j).wait_send()

    @pl.loop(0, UNITS)
    def _(s):
        for hop in range(2):
            f_copy(hop, s).wait_send()

    for dx in reversed(turns):
        for b in range(per_x):
            src = along(X - dx, b)

            def take(dx=dx, b=b, src=src):
                block = rbuf.at[src]
                remote(block, block, a_send.at[dx * per_x + b],
                       a_recv.at[dx * per_x + b], (src, f)).wait_recv()
                for r in range(ROUNDS):
                    out_ref[pl.ds(r * cap * G + src, cap, stride=G), :] = rbuf[src, r]

            other(src, dx, take)
    for dx in turns:
        for b in range(per_x):
            o, copy = a_copy(dx, b)
            other(o, dx, copy.wait_send)


def per_device(spectra, station_mask, owners):
    G = lax.axis_size("grp")
    F = lax.axis_size("freq")
    Y = F // Z
    cap = (2 * PAIRS + G - 1) // G
    capp = -(-cap // 8) * 8
    hbm = pl.BlockSpec(memory_space=pltpu.HBM)
    dma = pltpu.SemaphoreType.DMA
    vmem = pltpu.VMEM
    held = pl.pallas_call(
        functools.partial(kernel, (G, Y, cap, capp)),
        out_shape=jax.ShapeDtypeStruct((ROUNDS * cap * G, BINS), F32),
        in_specs=[hbm] * 3,
        out_specs=pl.BlockSpec(memory_space=vmem),
        scratch_shapes=[
            vmem((STA, 2, BINS), F32),
            vmem((1, STA), jnp.int32),
            vmem((ROUNDS, PAIRS), jnp.int32),
            vmem((ROUNDS, G * capp, PAIRS), BF16),
            vmem((2, F, BINS), F32),
            vmem((ROUNDS + 1, UNITS, Y // 2, 2, STA, BINS), F32),
            vmem((UNITS, Y * BINS, 2 * BINS), BF16),
            vmem((2 * ROUNDS * PAIRS, Y * BINS), BF16),
            vmem((2 * ROUNDS * PAIRS, 2 * BINS), F32),
            vmem((G, ROUNDS, cap, BINS), F32),
            vmem((G, ROUNDS, cap, BINS), F32),
            dma((3,)), dma((4,)), dma((4,)),
            dma((Z, Y)), dma((Z, Y)),
            dma((2, UNITS)), dma((2, UNITS)),
            dma((G,)), dma((G,)),
        ],
        compiler_params=pltpu.CompilerParams(
            collective_id=0, has_side_effects=True, vmem_limit_bytes=32 << 20),
    )(*(pltpu.with_memory_space_constraint(v, pltpu.HBM) for v in (spectra, station_mask.reshape(1, STA), owners.reshape(ROUNDS, PAIRS))))
    return held.reshape(1, ROUNDS, cap, G, BINS).transpose(0, 1, 3, 2, 4)


def solution(mesh):
    placed = (P("grp", None, "freq"), P("grp"), P("grp", None, None, None))
    return jax.shard_map(
        per_device,
        mesh=mesh,
        in_specs=placed,
        out_specs=P("grp", None, None, None, "freq"),
        check_vma=False,
    )
```

time: 45.4 us -> 42.6 us (0.938)
  Pallas kernels: 43.1 us -> 41.7 us
  local copies, waits for them, and re-layouts: 2.04 us -> 0.66 us
    unnamed x7 -> x1, local copies, waits for them, and re-layouts: 2.04 us -> 0.66 us
    pallas_call x1, Pallas kernels: 43.1 us -> 41.7 us  [per_device(): pl.pallas_call(functools.partial(kernel, (G, Y, cap, capp)), out_shape=ja...]
where the time goes in v3:
time: 42.6 us; the launch traced here: 42.4 us
  Pallas kernels  41.7 us (98%)
  local copies, waits for them, and re-layouts  0.66 us (2%)
    pallas_call x1, Pallas kernels, per_device(): pl.pallas_call(functools.partial(kernel, (G, Y, cap, capp)), out_shape=ja...  41.7 us

profile of v3, /device:TPU:1, one launch (start us, length us, event | category | flops | bytes accessed | tf_op | source)
XLA Modules:
  0.0 42.4 jit_solution(17135930385252096074)
XLA Ops:
  0.0 41.7 %shard_map.37 = f32[288,128]{1,0:T(8,128)S(1)} custom-call(f32[8,2,128]{2,1,0:T(2,128)} %x_hbm.1, s32[1,8]{1,0:T(1,128)} %bitcast.7, s32[2,64]{1,0:T(2,128)} %bitcast.6), custom_call_target="tpu_custom_call" | custom-call | tf_op jit(solution)/shard_map/pallas_call | solution.py:283
  41.8 0.7 %copy.5 = f32[1,2,24,6,128]{4,2,3,1,0:T(8,128)} copy(f32[1,2,24,6,128]{4,2,3,1,0:T(8,128)S(1)} %bitcast.5) | data formatting | bytes 294912

commit v4 on v3

--- a/solution.py
+++ b/solution.py
@@ -67,28 +67,29 @@
         else:
             do()
 
-    barrier = pltpu.get_barrier_semaphore()
-
-    def greet(peer):
-        pl.semaphore_signal(barrier, inc=1, device_id=peer, device_id_type=MESH)
-
-    greet(zpeer(1))
-    greet(zpeer(Z - 1))
-
-    @pl.loop(1, Y)
-    def _(d):
-        greet(ypeer(d))
-
-    @pl.loop(1, G)
-    def _(d):
-        greet((lax.rem(g + d, G), f))
-
     loads = [
         pltpu.make_async_copy(a, b, in_sem.at[i])
         for i, (a, b) in enumerate(((x_hbm, xin), (mask_hbm, maskin), (owner_hbm, ownerin)))]
     for load in loads:
         load.start()
 
+    barrier = pltpu.get_barrier_semaphore()
+
+    def greet(peer):
+        pl.semaphore_signal(barrier, inc=1, device_id=peer, device_id_type=MESH)
+
+    greet(zpeer(1))
+    greet(zpeer(Z - 1))
+
+    @pl.loop(1, Y)
+    def _(d):
+        greet(ypeer(d))
+
+    @pl.loop(1, G)
+    def _(d):
+        greet((lax.rem(g + d, G), f))
+
+
     for load in loads:
         load.wait()
 
@@ -115,10 +116,9 @@
         return remote(buf.at[0, 0, 0], buf.at[0, 2 * PLACE[d], 0],
                       z_send.at[PLACE[d] - 1], z_recv.at[PLACE[d] - 1], zpeer(d))
 
-    def z_relay(d):
-        part = 0 if d == 1 else 1
-        return remote(buf.at[0, 2 * PLACE[d], 0, part], buf.at[0, 2 * PLACE[2], 0, part],
-                      z_send.at[2 + part], z_recv.at[2 + part], zpeer(d))
+    def z_relay():
+        return remote(buf.at[0, 2 * PLACE[Z - 1], 0], buf.at[0, 2 * PLACE[2], 0],
+                      z_send.at[2], z_recv.at[2], zpeer(Z - 1))
 
     def y_copy(e, j):
         i = 2 * j if j < Y // 2 else 2 * (Y - j) - 1
@@ -163,9 +163,9 @@
 
     pl.loop(0, UNITS // 2)(table)
     acc[...] = jnp.zeros_like(acc)
-    for d in (1, Z - 1):
-        z_copy(d).wait_recv()
-        z_relay(d).start()
+    z_copy(Z - 1).wait_recv()
+    z_relay().start()
+    z_copy(1).wait_recv()
     for d in (1, Z - 1):
         for j in rows:
             y_copy(PLACE[d], j).start()
@@ -196,12 +196,11 @@
                     xb[(2 * r + 1) * PAIRS:(2 * r + 2) * PAIRS, at:at + BINS] = lo
         acc[...] += jnp.dot(xb[...], tab[s], preferred_element_type=F32)
 
-    @pl.loop(0, UNITS + LAG)
+    @pl.loop(0, UNITS + LAG + 1)
     def _(t):
         @pl.when(t == 2)
         def _():
-            for d in (1, Z - 1):
-                z_relay(d).wait_recv()
+            z_relay().wait_recv()
             for j in rows:
                 y_copy(PLACE[2], j).start()
 
@@ -217,14 +216,15 @@
                     pl.when(lax.rem(t, 2) == 1)(arrive)
                 else:
                     arrive()
+            f_copy(1, t).start()
             f_copy(0, t).start()
-            f_copy(1, t).start()
-
-        @pl.when(t >= LAG)
+
+        @pl.when((t >= LAG) & (t != UNITS - 2))
         def _():
-            f_copy(0, t - LAG).wait_recv()
-            f_copy(1, t - LAG).wait_recv()
-            product(t - LAG)
+            u = t - LAG - jnp.where(t > UNITS - 2, 1, 0)
+            f_copy(0, u).wait_recv()
+            f_copy(1, u).wait_recv()
+            product(u)
 
     for r in range(ROUNDS):
         top, low = 2 * r * PAIRS, (2 * r + 1) * PAIRS
@@ -243,7 +243,7 @@
 
     for d in (1, Z - 1):
         z_copy(d).wait_send()
-        z_relay(d).wait_send()
+    z_relay().wait_send()
     for e in range(Z):
         for j in rows:
             y_copy(e, j).wait_send()
@@ -297,7 +297,7 @@
             vmem((2 * ROUNDS * PAIRS, 2 * BINS), F32),
             vmem((G, ROUNDS, cap, BINS), F32),
             vmem((G, ROUNDS, cap, BINS), F32),
-            dma((3,)), dma((4,)), dma((4,)),
+            dma((3,)), dma((3,)), dma((3,)),
             dma((Z, Y)), dma((Z, Y)),
             dma((2, UNITS)), dma((2, UNITS)),
             dma((G,)), dma((G,)),

time: 42.6 us -> 42.1 us (0.988)
  Pallas kernels: 41.7 us -> 41.2 us
    pallas_call x1, Pallas kernels: 41.7 us -> 41.2 us  [per_device(): pl.pallas_call(functools.partial(kernel, (G, Y, cap, capp)), out_shape=ja...]
where the time goes in v4:
time: 42.1 us; the launch traced here: 41.9 us
  Pallas kernels  41.2 us (98%)
  local copies, waits for them, and re-layouts  0.66 us (2%)
    pallas_call x1, Pallas kernels, per_device(): pl.pallas_call(functools.partial(kernel, (G, Y, cap, capp)), out_shape=ja...  41.2 us

profile of v4, /device:TPU:1, one launch (start us, length us, event | category | flops | bytes accessed | tf_op | source)
XLA Modules:
  0.0 41.9 jit_solution(5614564867007927874)
XLA Ops:
  0.0 41.2 %shard_map.37 = f32[288,128]{1,0:T(8,128)S(1)} custom-call(f32[8,2,128]{2,1,0:T(2,128)} %x_hbm.1, s32[1,8]{1,0:T(1,128)} %bitcast.7, s32[2,64]{1,0:T(2,128)} %bitcast.6), custom_call_target="tpu_custom_call" | custom-call | tf_op jit(solution)/shard_map/pallas_call | solution.py:283
  41.3 0.7 %copy.5 = f32[1,2,24,6,128]{4,2,3,1,0:T(8,128)} copy(f32[1,2,24,6,128]{4,2,3,1,0:T(8,128)S(1)} %bitcast.5) | data formatting | bytes 294912

commit v5 on v4

--- a/solution.py
+++ b/solution.py
@@ -90,7 +90,7 @@
         greet((lax.rem(g + d, G), f))
 
 
-    for load in loads:
+    for load in loads[:2]:
         load.wait()
 
     def column(row):
@@ -171,6 +171,7 @@
             y_copy(PLACE[d], j).start()
     pl.loop(UNITS // 2, UNITS)(table)
 
+    loads[2].wait()
     for r in range(ROUNDS):
         row = ownerin[r:r + 1, :].astype(F32)
         ahead = lax.broadcasted_iota(jnp.int32, (PAIRS, PAIRS), 0) < lax.broadcasted_iota(

time: 42.1 us -> 42.1 us (level)
  no operation moved by 1% of the time
where the time goes in v5:
time: 42.1 us; the launch traced here: 41.9 us
  Pallas kernels  41.2 us (98%)
  local copies, waits for them, and re-layouts  0.66 us (2%)
    pallas_call x1, Pallas kernels, per_device(): pl.pallas_call(functools.partial(kernel, (G, Y, cap, capp)), out_shape=ja...  41.2 us

profile of v5, /device:TPU:1, one launch (start us, length us, event | category | flops | bytes accessed | tf_op | source)
XLA Modules:
  0.0 41.9 jit_solution(12229697968860371373)
XLA Ops:
  0.0 41.2 %shard_map.37 = f32[288,128]{1,0:T(8,128)S(1)} custom-call(f32[8,2,128]{2,1,0:T(2,128)} %x_hbm.1, s32[1,8]{1,0:T(1,128)} %bitcast.7, s32[2,64]{1,0:T(2,128)} %bitcast.6), custom_call_target="tpu_custom_call" | custom-call | tf_op jit(solution)/shard_map/pallas_call | solution.py:284
  41.3 0.7 %copy.5 = f32[1,2,24,6,128]{4,2,3,1,0:T(8,128)} copy(f32[1,2,24,6,128]{4,2,3,1,0:T(8,128)S(1)} %bitcast.5) | data formatting | bytes 294912

commit v6 on v5

--- a/solution.py
+++ b/solution.py
@@ -165,10 +165,11 @@
     acc[...] = jnp.zeros_like(acc)
     z_copy(Z - 1).wait_recv()
     z_relay().start()
+    for j in rows:
+        y_copy(PLACE[Z - 1], j).start()
     z_copy(1).wait_recv()
-    for d in (1, Z - 1):
-        for j in rows:
-            y_copy(PLACE[d], j).start()
+    for j in rows:
+        y_copy(PLACE[1], j).start()
     pl.loop(UNITS // 2, UNITS)(table)
 
     loads[2].wait()

time: 42.1 us -> 42.2 us (level)
  no operation moved by 1% of the time
where the time goes in v6:
time: 42.2 us; the launch traced here: 42 us
  Pallas kernels  41.3 us (98%)
  local copies, waits for them, and re-layouts  0.66 us (2%)
    pallas_call x1, Pallas kernels, per_device(): pl.pallas_call(functools.partial(kernel, (G, Y, cap, capp)), out_shape=ja...  41.3 us

profile of v6, /device:TPU:1, one launch (start us, length us, event | category | flops | bytes accessed | tf_op | source)
XLA Modules:
  0.0 42.0 jit_solution(15834034049477441172)
XLA Ops:
  0.0 41.3 %shard_map.37 = f32[288,128]{1,0:T(8,128)S(1)} custom-call(f32[8,2,128]{2,1,0:T(2,128)} %x_hbm.1, s32[1,8]{1,0:T(1,128)} %bitcast.7, s32[2,64]{1,0:T(2,128)} %bitcast.6), custom_call_target="tpu_custom_call" | custom-call | tf_op jit(solution)/shard_map/pallas_call | solution.py:285
  41.4 0.7 %copy.5 = f32[1,2,24,6,128]{4,2,3,1,0:T(8,128)} copy(f32[1,2,24,6,128]{4,2,3,1,0:T(8,128)S(1)} %bitcast.5) | data formatting | bytes 294912
